TPU v7x, 32 devices: a whole 2x2x4 slice. The times are simulated.
32 devices in a mesh: wide: 8 (over y, x, core), narrow: 4 (over z).
Axes of the slice: x: 2, y: 2, z: 4, core: 2. Of those that a mesh axis runs over, the one named last changes fastest.
Arguments:
- batch_index: int32 [256], P('narrow'), may hold values from 0 to 255
- train_features: float32 [1024, 1024], P('narrow'), may hold values from -6 to 6
- train_labels: float32 [1024, 1000], P('narrow'), may hold values from -12 to 12
- centers: float32 [8192, 1024], P(('wide', 'narrow')), may hold values from -6 to 6
- weights: float32 [8192, 1000], P(('wide', 'narrow')), may hold values from -6 to 6
Outputs:
- new_weights: float32 [8192, 1000], P(('wide', 'narrow'))
- residual: float32 [256, 1000], P('narrow')
Inputs may be any that keep to these rules, and one draw needn't show every extreme that they name: `batch_index`: entry i names a row of the training shard held by narrow index i // 64.
All inputs are finite; a program needn't handle non-finite values.
Results may differ from a plain program's by a relative error of at most 0.0001.
Values sent between devices are 32-bit elements; how exact they have to be, the bound alone decides.
A program may use at most 64 MiB of HBM per device.

v0:
```python
import math
import jax
import jax.numpy as jnp
from jax import lax
from jax.sharding import PartitionSpec as P

step_size = 1.0


def per_device(batch_index, train_features, train_labels, centers, weights):
    rows = jnp.take(train_features, batch_index, axis=0)
    targets = jnp.take(train_labels, batch_index, axis=0)
    features = centers.shape[1]
    center_sq = jnp.sum(centers * centers, axis=1)
    count = centers.shape[0] * lax.axis_size("wide") * lax.axis_size("narrow")
    scale = 1.0 / math.sqrt(count)
    piece = lax.all_gather(rows, "narrow", axis=0, tiled=True)
    inner = jnp.dot(
        piece, centers.T, precision=lax.Precision.HIGHEST, preferred_element_type=jnp.float32
    )
    piece_sq = jnp.sum(piece * piece, axis=1)
    kernel = jnp.exp(
        (2.0 * features - piece_sq[:, None] - center_sq[None, :] + 2.0 * inner) / 128.0
    )
    batch = kernel.shape[0]
    kern_rows = kernel
    local = lax.psum_scatter(
        jnp.dot(
            kern_rows, weights, precision=lax.Precision.HIGHEST, preferred_element_type=jnp.float32
        ),
        "narrow",
        scatter_dimension=0,
        tiled=True,
    )
    predicted = lax.psum(local, "wide") * scale
    residual = predicted - targets
    kern_rows = kernel
    delta = lax.dot_general(
        kern_rows,
        lax.all_gather(residual, "narrow", axis=0, tiled=True),
        (((0,), (0,)), ((), ())),
        precision=lax.Precision.HIGHEST,
        preferred_element_type=jnp.float32,
    )
    new_weights = weights - step_size / batch * delta
    return (new_weights, residual)


def solution(mesh):
    in_specs = (
        P("narrow"),
        P("narrow", None),
        P("narrow", None),
        P(("wide", "narrow"), None),
        P(("wide", "narrow"), None),
    )
    out_specs = (P(("wide", "narrow"), None), P("narrow", None))
    return jax.shard_map(
        per_device, mesh=mesh, in_specs=in_specs, out_specs=out_specs, check_vma=False
    )
```

profile of v0, /device:TPU:0, one launch (start us, length us, event | category | flops | bytes accessed | tf_op | source)
XLA Modules:
  0.0 160.9 jit_solution(7561517133553205740)
XLA Ops:
  7.2 0.0 copy-start
  7.2 0.0 copy-start.5
  7.2 0.0 all-gather.2.cloned.1.call-start
  7.2 0.7 compare_and_fusion
  8.0 0.0 copy-done.5
  8.0 0.4 copy-done
  8.4 0.0 copy-start.1
  8.4 0.7 gather_fusion
  9.1 0.8 broadcast_select_fusion
  9.9 0.0 all-gather.2.cloned.1.call-update
  9.9 0.0 reduce-scatter.2.cloned.1.call-start
  10.0 0.0 copy-done.1
  10.0 0.1 multiply_reduce_fusion
  10.1 30.7 %all-gather.2.cloned.1.call-done = f32[256,1024]{1,0:T(8,128)} async-done(((f32[64,1024]{1,0:T(8,128)}), f32[256,1024]{1,0:T(8,128)}) %all-gather.2.cloned.1.call-update) | async-done | bytes 1048592 | tf_op jit(solution)/shard_map/all_gather | solution.py:17
  40.9 0.0 copy-start.2
  40.9 1.5 multiply_reduce_fusion.1
  42.4 0.1 copy-done.2
  42.4 0.0 copy-start.3
  42.4 1.1 fusion.3
  43.5 0.1 copy-done.3
  43.6 2.0 %fusion.4 = f32[256,1000]{1,0:T(8,128)} fusion(f32[256,256]{1,0:T(8,128)S(1)} %fusion.3, f32[256,1000]{0,1:T(8,128)S(1)} %copy-done.3), kind=kOutput, calls=%fused_computation.16 | convolution fusion | flops 786432000 | bytes 2310144 | tf_op jit(solution)/shard_map/dot_general | solution.py:28
  45.7 0.0 reduce-scatter.2.cloned.1.call-update
  45.7 0.0 all-reduce.2.cloned.1.call-start
  45.7 26.8 %reduce-scatter.2.cloned.1.call-done = f32[64,1000]{1,0:T(8,128)} async-done(((f32[256,1000]{1,0:T(8,128)}), f32[64,1000]{1,0:T(8,128)}) %reduce-scatter.2.cloned.1.call-update) | async-done | bytes 256016 | tf_op jit(solution)/shard_map/reduce_scatter | solution.py:27
  72.5 0.0 all-reduce.2.cloned.1.call-update
  72.5 1.5 copy.7
  74.1 1.4 gather_fusion.1
  75.5 52.5 %all-reduce.2.cloned.1.call-done = f32[64,1000]{1,0:T(8,128)} async-done(((f32[64,1000]{1,0:T(8,128)}), f32[64,1000]{1,0:T(8,128)}) %all-reduce.2.cloned.1.call-update) | async-done | bytes 256016 | tf_op jit(solution)/shard_map/psum | solution.py:35
  128.0 1.1 select_subtract_fusion
  129.1 0.0 copy-start.4
  129.1 22.5 %all_gather.7 = f32[256,1000]{1,0:T(8,128)S(1)} all-gather(f32[64,1000]{1,0:T(8,128)S(1)} %select_subtract_fusion), channel_id=1, replica_groups=mesh['wide'=8,'narrow'=4] {'narrow'}, dimensions={0}, use_global_device_ids=true | all-gather | bytes 1280000 | tf_op jit(solution)/shard_map/all_gather | solution.py:40
  151.6 0.0 copy-done.4
  151.6 2.8 %fusion = f32[256,1000]{0,1:T(8,128)} fusion(f32[256,1000]{0,1:T(8,128)S(1)} %copy-done.3, f32[256,256]{1,0:T(8,128)S(1)} %fusion.3, f32[256,1000]{1,0:T(8,128)S(1)} %all_gather.7), kind=kOutput, calls=%fused_computation.3 | convolution fusion | flops 786944000 | bytes 3334144 | tf_op jit(solution)/shard_map/dot_general | solution.py:38
  (3 shorter events, 0.0 us)
Async XLA Ops:
  7.2 1.3 copy-start
  7.2 0.8 copy-start.5
  7.2 33.7 %all-gather.2.cloned.1.call-start = ((), (), s32[]{:S(2)}) async-start(), calls=%async_computation.1 | async-start | bytes 1310720 | tf_op jit(solution)/shard_map/all_gather | solution.py:17
  8.4 1.6 copy-start.1
  9.9 62.6 %reduce-scatter.2.cloned.1.call-start = ((), (), s32[]{:S(2)}) async-start(), calls=%async_computation.2 | async-start | bytes 1310720 | tf_op jit(solution)/shard_map/reduce_scatter | solution.py:27
  40.9 1.5 copy-start.2
  42.4 1.2 copy-start.3
  45.7 82.3 %all-reduce.2.cloned.1.call-start = ((), (), s32[]{:S(2)}) async-start(), calls=%async_computation.3 | async-start | bytes 524288 | tf_op jit(solution)/shard_map/psum | solution.py:35
  129.1 22.5 %copy-start.4 = (f32[64,1000]{1,0:T(8,128)}, f32[64,1000]{1,0:T(8,128)S(1)}, u32[]{:S(2)}) copy-start(f32[64,1000]{1,0:T(8,128)S(1)} %select_subtract_fusion) | copy-start | bytes 768004
Sparse Core Ops, SparseCore 0:
  10.1 30.6 all-gather.1
  45.8 26.6 reduce-scatter.1
  75.6 52.3 all-reduce.1
where the time goes:
time: 161 us
  waiting for transfers between devices  110 us (68%)
  blocking collectives  22.5 us (14%)
  between operations  13.8 us (9%)
  matrix products  5.91 us (4%)
  other arithmetic  4.28 us (3%)
  local copies, waits for them, and re-layouts  4.26 us (3%)
    psum x1, waiting for transfers between devices, per_device(): predicted = lax.psum(local, 'wide') * scale  52.5 us
    all_gather x1, waiting for transfers between devices, per_device(): piece = lax.all_gather(rows, 'narrow', axis=0, tiled=True)  30.7 us
    reduce_scatter x1, waiting for transfers between devices, per_device(): lax.psum_scatter(jnp.dot(kern_rows, weights, precision=lax.Precision.HIGH...  26.8 us
    all_gather x1, blocking collectives, per_device(): lax.all_gather(residual, 'narrow', axis=0, tiled=True)  22.5 us
  transfers between devices with their start and end apart: 3, of which 3 were waited for; matrix products, arithmetic and copies ran while one was open for 2% of the time, Pallas kernels for 0%

commit v1 on v0

--- a/solution.py
+++ b/solution.py
@@ -32,7 +32,7 @@
         scatter_dimension=0,
         tiled=True,
     )
-    predicted = lax.psum(local, "wide") * scale
+    predicted = jnp.sum(lax.all_gather(local, "wide"), axis=0) * scale
     residual = predicted - targets
     kern_rows = kernel
     delta = lax.dot_general(

time: 161 us -> 136 us (0.84)
  waiting for transfers between devices: 110 us -> 82.7 us
    psum x1 -> x0, waiting for transfers between devices: 52.5 us -> none  [per_device(): predicted = lax.psum(local, 'wide') * scale]
    all_gather x0 -> x1, waiting for transfers between devices: none -> 25.2 us  [per_device(): predicted = jnp.sum(lax.all_gather(local, 'wide'), axis=0) * scale]
    reduce_sum x0 -> x1, other arithmetic: none -> 1.76 us  [per_device(): predicted = jnp.sum(lax.all_gather(local, 'wide'), axis=0) * scale]
where the time goes in v1:
time: 136 us
  waiting for transfers between devices  82.7 us (61%)
  blocking collectives  22.5 us (17%)
  between operations  13.8 us (10%)
  matrix products  7.13 us (5%)
  other arithmetic  5.64 us (4%)
  local copies, waits for them, and re-layouts  3.63 us (3%)
    all_gather x1, waiting for transfers between devices, per_device(): piece = lax.all_gather(rows, 'narrow', axis=0, tiled=True)  30.6 us
    reduce_scatter x1, waiting for transfers between devices, per_device(): lax.psum_scatter(jnp.dot(kern_rows, weights, precision=lax.Precision.HIGH...  26.8 us
    all_gather x1, waiting for transfers between devices, per_device(): predicted = jnp.sum(lax.all_gather(local, 'wide'), axis=0) * scale  25.2 us
    all_gather x1, blocking collectives, per_device(): lax.all_gather(residual, 'narrow', axis=0, tiled=True)  22.5 us
    dot_general x1, matrix products, per_device(): lax.dot_general(kern_rows, lax.all_gather(residual, 'narrow', axis=0, til...  2.82 us
  transfers between devices with their start and end apart: 3, of which 3 were waited for; matrix products, arithmetic and copies ran while one was open for 2% of the time, Pallas kernels for 0%

profile of v1, /device:TPU:0, one launch (start us, length us, event | category | flops | bytes accessed | tf_op | source)
XLA Modules:
  0.0 135.6 jit_solution(15014058737612504367)
XLA Ops:
  7.2 0.0 copy-start
  7.2 0.0 copy-start.1
  7.2 0.0 all-gather.4.cloned.1.call-start
  7.2 0.8 compare_and_fusion
  8.0 0.7 compare_select_fusion
  8.7 0.0 copy-done
  8.7 0.7 gather_fusion
  9.4 0.8 broadcast_select_fusion
  10.2 0.0 all-gather.4.cloned.1.call-update
  10.2 0.0 copy-start.2
  10.2 0.0 reduce-scatter.2.cloned.1.call-start
  10.3 0.0 copy-done.1
  10.3 0.1 multiply_reduce_fusion
  10.4 30.6 %all-gather.4.cloned.1.call-done = f32[256,1024]{1,0:T(8,128)} async-done(((f32[64,1024]{1,0:T(8,128)}), f32[256,1024]{1,0:T(8,128)}) %all-gather.4.cloned.1.call-update) | async-done | bytes 1048592 | tf_op jit(solution)/shard_map/all_gather | solution.py:17
  41.1 1.4 %multiply_reduce_fusion.1 = f32[256]{0:T(256)S(1)} fusion(f32[256,1024]{1,0:T(8,128)} %all-gather.4.cloned.1.call-done), kind=kLoop, calls=%fused_computation.9 | loop fusion | flops 524032 | bytes 1049600 | tf_op jit(solution)/shard_map/reduce_sum | solution.py:21
  42.4 2.3 %fusion.3 = f32[256,256]{1,0:T(8,128)S(1)} fusion(f32[256,1024]{1,0:T(8,128)} %all-gather.4.cloned.1.call-done, f32[256,1024]{1,0:T(8,128)S(1)} %copy-done.1, f32[256]{0:T(256)S(1)} %multiply_reduce_fusion, f32[256]{0:T(256)S(1)} %broadcast_subtract_fusion), kind=kOutput, calls=%fused_computation.7 | convolution fusion | flops 805568512 | bytes 2361344 | tf_op jit(solution)/shard_map/dot_general | solution.py:18
  44.7 0.0 copy-done.2
  44.7 2.0 %fusion.4 = f32[256,1000]{1,0:T(8,128)} fusion(f32[256,256]{1,0:T(8,128)S(1)} %fusion.3, f32[256,1000]{0,1:T(8,128)S(1)} %copy-done.2), kind=kOutput, calls=%fused_computation.16 | convolution fusion | flops 786432000 | bytes 2310144 | tf_op jit(solution)/shard_map/dot_general | solution.py:28
  46.8 0.0 reduce-scatter.2.cloned.1.call-update
  46.8 0.0 all-gather.6.cloned.1.call-start
  46.9 26.8 %reduce-scatter.2.cloned.1.call-done = f32[64,1000]{1,0:T(8,128)} async-done(((f32[256,1000]{1,0:T(8,128)}), f32[64,1000]{1,0:T(8,128)}) %reduce-scatter.2.cloned.1.call-update) | async-done | bytes 256016 | tf_op jit(solution)/shard_map/reduce_scatter | solution.py:27
  73.6 0.0 all-gather.6.cloned.1.call-update
  73.7 1.5 %copy.7 = f32[256,1000]{1,0:T(8,128)S(1)} copy(f32[256,1000]{0,1:T(8,128)} %param.7) | data formatting | bytes 2048000 | tf_op args[2]
  75.2 1.4 %gather_fusion.1 = f32[64,1000]{1,0:T(8,128)} fusion(f32[256,1000]{1,0:T(8,128)S(1)} %copy.7, s32[1024]{0:T(1024)S(1)} %pad_clamp_fusion), kind=kCustom, calls=%fused_computation.1 | custom fusion | bytes 512256 | tf_op jit(solution)/shard_map/jit(_take)/gather | solution.py:12
  76.6 0.0 copy-start.4
  76.6 25.2 %all-gather.6.cloned.1.call-done = f32[512,1000]{1,0:T(8,128)} async-done(((f32[64,1000]{1,0:T(8,128)}), f32[512,1000]{1,0:T(8,128)}) %all-gather.6.cloned.1.call-update) | async-done | bytes 2048016 | tf_op jit(solution)/shard_map/all_gather | solution.py:35
  101.8 1.8 %reduce_sum.29 = f32[64,1000]{1,0:T(8,128)S(1)} reduce(f32[8,64,1000]{2,1,0:T(8,128)} %bitcast.7, f32[]{:T(128)} %constant.36.clone.1), dimensions={0}, to_apply=%region_3.4 | reduce | flops 448000 | bytes 2304004 | tf_op jit(solution)/shard_map/reduce_sum | solution.py:35
  103.6 0.0 copy-done.4
  103.6 0.1 select_subtract_fusion
  103.7 0.0 copy-start.3
  103.7 22.5 %all_gather.15 = f32[256,1000]{1,0:T(8,128)S(1)} all-gather(f32[64,1000]{1,0:T(8,128)S(1)} %select_subtract_fusion), channel_id=1, replica_groups=mesh['wide'=8,'narrow'=4] {'narrow'}, dimensions={0}, use_global_device_ids=true | all-gather | bytes 1280000 | tf_op jit(solution)/shard_map/all_gather | solution.py:40
  126.2 2.8 %fusion = f32[256,1000]{0,1:T(8,128)} fusion(f32[256,1000]{0,1:T(8,128)S(1)} %copy-done.2, f32[256,256]{1,0:T(8,128)S(1)} %fusion.3, f32[256,1000]{1,0:T(8,128)S(1)} %all_gather.15), kind=kOutput, calls=%fused_computation.3 | convolution fusion | flops 786944000 | bytes 3334144 | tf_op jit(solution)/shard_map/dot_general | solution.py:38
  129.1 0.0 copy-done.3
  (2 shorter events, 0.0 us)
Async XLA Ops:
  7.2 1.5 %copy-start = (f32[256,1024]{1,0:T(8,128)S(1)}, f32[256,1024]{1,0:T(8,128)}, u32[]{:S(2)}) copy-start(f32[256,1024]{1,0:T(8,128)} %param.6) | copy-start | bytes 3145732
  7.2 3.1 %copy-start.1 = (f32[256,1024]{1,0:T(8,128)S(1)}, f32[256,1024]{1,0:T(8,128)}, u32[]{:S(2)}) copy-start(f32[256,1024]{1,0:T(8,128)} %param.8) | copy-start | bytes 3145732
  7.2 33.9 %all-gather.4.cloned.1.call-start = ((), (), s32[]{:S(2)}) async-start(), calls=%async_computation.1 | async-start | bytes 1310720 | tf_op jit(solution)/shard_map/all_gather | solution.py:17
  10.2 34.5 %copy-start.2 = (f32[256,1000]{0,1:T(8,128)S(1)}, f32[256,1000]{0,1:T(8,128)}, u32[]{:S(2)}) copy-start(f32[256,1000]{0,1:T(8,128)} %param.9) | copy-start | bytes 3072004
  10.2 63.4 %reduce-scatter.2.cloned.1.call-start = ((), (), s32[]{:S(2)}) async-start(), calls=%async_computation.2 | async-start | bytes 1310720 | tf_op jit(solution)/shard_map/reduce_scatter | solution.py:27
  46.8 55.0 %all-gather.6.cloned.1.call-start = ((), (), s32[]{:S(2)}) async-start(), calls=%async_computation.3 | async-start | bytes 2359296 | tf_op jit(solution)/shard_map/all_gather | solution.py:35
  76.6 27.0 %copy-start.4 = (f32[64,1000]{1,0:T(8,128)S(1)}, f32[64,1000]{1,0:T(8,128)}, u32[]{:S(2)}) copy-start(f32[64,1000]{1,0:T(8,128)} %gather_fusion.1) | copy-start | bytes 768004
  103.7 25.4 %copy-start.3 = (f32[64,1000]{1,0:T(8,128)}, f32[64,1000]{1,0:T(8,128)S(1)}, u32[]{:S(2)}) copy-start(f32[64,1000]{1,0:T(8,128)S(1)} %select_subtract_fusion) | copy-start | bytes 768004
Sparse Core Ops, SparseCore 0:
  10.3 30.6 all-gather.3
  46.9 26.6 reduce-scatter.1
  75.5 26.2 all-gather.5

commit v2 on v0

--- a/solution.py
+++ b/solution.py
@@ -14,7 +14,14 @@
     center_sq = jnp.sum(centers * centers, axis=1)
     count = centers.shape[0] * lax.axis_size("wide") * lax.axis_size("narrow")
     scale = 1.0 / math.sqrt(count)
-    piece = lax.all_gather(rows, "narrow", axis=0, tiled=True)
+    ring = [rows]
+    for hop in range(3):
+        ring.append(lax.ppermute(ring[-1], "narrow", [(dev, (dev + 1) % 4) for dev in range(4)]))
+    piece = jnp.roll(
+        jnp.concatenate(ring[::-1], axis=0),
+        (lax.axis_index("narrow") + 1) * ring[0].shape[0],
+        axis=0,
+    )
     inner = jnp.dot(
         piece, centers.T, precision=lax.Precision.HIGHEST, preferred_element_type=jnp.float32
     )

time: 161 us -> 156 us (0.969)
  waiting for transfers between devices: 110 us -> 104 us
  starting transfers between devices: 0.12 us -> 3.19 us
    all_gather x1 -> x0, waiting for transfers between devices: 30.7 us -> none  [per_device(): piece = lax.all_gather(rows, 'narrow', axis=0, tiled=True)]
    ppermute x0 -> x3, waiting for transfers between devices: none -> 25.9 us  [per_device(): lax.ppermute(ring[-1], 'narrow', [(dev, (dev + 1) % 4) for dev in range(4)])]
    ppermute x0 -> x3, starting transfers between devices: none -> 3.11 us  [per_device(): lax.ppermute(ring[-1], 'narrow', [(dev, (dev + 1) % 4) for dev in range(4)])]
    reduce_scatter x1, waiting for transfers between devices: 26.8 us -> 25.2 us  [per_device(): lax.psum_scatter(jnp.dot(kern_rows, weights, precision=lax.Precision.HIGH...]
  transfers between devices with their start and end apart: 3 -> 5, of which waited for: 3 -> 5; matrix products, arithmetic and copies ran while one was open for 2% -> 2% of each run, Pallas kernels for 0% -> 0%
where the time goes in v2:
time: 156 us
  waiting for transfers between devices  104 us (67%)
  blocking collectives  22.5 us (14%)
  between operations  14.2 us (9%)
  matrix products  5.85 us (4%)
  local copies, waits for them, and re-layouts  3.75 us (2%)
  starting transfers between devices  3.19 us (2%)
  other arithmetic  3.16 us (2%)
    psum x1, waiting for transfers between devices, per_device(): predicted = lax.psum(local, 'wide') * scale  52.5 us
    ppermute x3, waiting for transfers between devices, per_device(): lax.ppermute(ring[-1], 'narrow', [(dev, (dev + 1) % 4) for dev in range(4)])  25.9 us
    reduce_scatter x1, waiting for transfers between devices, per_device(): lax.psum_scatter(jnp.dot(kern_rows, weights, precision=lax.Precision.HIGH...  25.2 us
    all_gather x1, blocking collectives, per_device(): lax.all_gather(residual, 'narrow', axis=0, tiled=True)  22.5 us
  transfers between devices with their start and end apart: 5, of which 5 were waited for; matrix products, arithmetic and copies ran while one was open for 2% of the time, Pallas kernels for 0%

profile of v2, /device:TPU:0, one launch (start us, length us, event | category | flops | bytes accessed | tf_op | source)
XLA Modules:
  0.0 156.2 jit_solution(16007714230651318189)
XLA Ops:
  7.2 0.0 copy-start
  7.2 0.0 copy-start.1
  7.2 0.0 reduce-scatter.2.cloned.1.call-start
  7.2 0.8 compare_select_fusion
  8.0 0.7 compare_and_fusion
  8.7 0.0 copy-done
  8.7 0.7 gather_fusion
  9.4 0.1 broadcast_select_fusion
  9.5 3.1 %collective-permute-start = (f32[64,1024]{1,0:T(8,128)S(1)}, f32[64,1024]{1,0:T(8,128)S(1)}, u32[]{:S(2)}, u32[]{:S(2)}) collective-permute-start(f32[64,1024]{1,0:T(8,128)S(1)} %broadcast_select_fusion), channel_id=1, source_target_pairs={{0,1},{1,2},{2,3},{3,0},{4,5},{5,6},{6,7},{7,4},{8,9},{9,10},{10,1... | collective-permute-start | bytes 786440 | tf_op jit(solution)/shard_map/ppermute | solution.py:19
  12.6 8.3 %collective-permute-done = f32[64,1024]{1,0:T(8,128)S(1)} collective-permute-done((f32[64,1024]{1,0:T(8,128)S(1)}, f32[64,1024]{1,0:T(8,128)S(1)}, u32[]{:S(2)}, u32[]{:S(2)}) %collective-permute-start) | collective-permute-done | bytes 262176 | tf_op jit(solution)/shard_map/ppermute | solution.py:19
  20.9 0.0 collective-permute-start.1
  20.9 9.3 %collective-permute-done.1 = f32[64,1024]{1,0:T(8,128)S(1)} collective-permute-done((f32[64,1024]{1,0:T(8,128)S(1)}, f32[64,1024]{1,0:T(8,128)S(1)}, u32[]{:S(2)}, u32[]{:S(2)}) %collective-permute-start.1) | collective-permute-done | bytes 262176 | tf_op jit(solution)/shard_map/ppermute | solution.py:19
  30.2 0.0 collective-permute-start.2
  30.2 0.0 copy-done.1
  30.2 0.1 multiply_reduce_fusion
  30.3 8.3 %collective-permute-done.2 = f32[64,1024]{1,0:T(8,128)S(1)} collective-permute-done((f32[64,1024]{1,0:T(8,128)S(1)}, f32[64,1024]{1,0:T(8,128)S(1)}, u32[]{:S(2)}, u32[]{:S(2)}) %collective-permute-start.2) | collective-permute-done | bytes 262176 | tf_op jit(solution)/shard_map/ppermute | solution.py:19
  38.7 0.1 constant_dynamic-update-slice_fusion.4
  38.9 0.0 copy-start.2
  38.9 0.1 constant_dynamic-update-slice_fusion
  39.0 0.2 multiply_reduce_fusion.1
  39.1 1.1 fusion.3
  40.2 0.0 copy-done.2
  40.2 0.0 copy-start.3
  40.2 2.0 %fusion.6 = f32[256,1000]{1,0:T(8,128)} fusion(f32[256,256]{1,0:T(8,128)S(1)} %fusion.3, f32[256,1000]{0,1:T(8,128)S(1)} %copy-done.2), kind=kOutput, calls=%fused_computation.26 | convolution fusion | flops 786432000 | bytes 2310144 | tf_op jit(solution)/shard_map/dot_general | solution.py:35
  42.2 0.0 reduce-scatter.2.cloned.1.call-update
  42.3 0.0 all-reduce.2.cloned.1.call-start
  42.3 25.2 %reduce-scatter.2.cloned.1.call-done = f32[64,1000]{1,0:T(8,128)} async-done(((f32[256,1000]{1,0:T(8,128)}), f32[64,1000]{1,0:T(8,128)}) %reduce-scatter.2.cloned.1.call-update) | async-done | bytes 256016 | tf_op jit(solution)/shard_map/reduce_scatter | solution.py:34
  67.5 0.0 copy-done.3
  67.5 0.0 all-reduce.2.cloned.1.call-update
  67.5 1.5 copy.7
  69.0 0.0 copy-start.4
  69.1 1.4 gather_fusion.1
  70.4 52.5 %all-reduce.2.cloned.1.call-done = f32[64,1000]{1,0:T(8,128)} async-done(((f32[64,1000]{1,0:T(8,128)}), f32[64,1000]{1,0:T(8,128)}) %all-reduce.2.cloned.1.call-update) | async-done | bytes 256016 | tf_op jit(solution)/shard_map/psum | solution.py:42
  122.9 1.1 select_subtract_fusion
  124.1 0.0 copy-start.5
  124.1 22.5 %all_gather.3 = f32[256,1000]{1,0:T(8,128)S(1)} all-gather(f32[64,1000]{1,0:T(8,128)S(1)} %select_subtract_fusion), channel_id=1, replica_groups=mesh['wide'=8,'narrow'=4] {'narrow'}, dimensions={0}, use_global_device_ids=true | all-gather | bytes 1280000 | tf_op jit(solution)/shard_map/all_gather | solution.py:47
  146.5 0.0 copy-done.4
  146.5 2.8 %fusion = f32[256,1000]{0,1:T(8,128)} fusion(f32[256,1000]{0,1:T(8,128)S(1)} %copy-done.2, f32[256,256]{1,0:T(8,128)S(1)} %copy-done.4, f32[256,1000]{1,0:T(8,128)S(1)} %all_gather.3), kind=kOutput, calls=%fused_computation.3 | convolution fusion | flops 786944000 | bytes 3334144 | tf_op jit(solution)/shard_map/dot_general | solution.py:45
  149.3 0.0 copy-done.5
  (8 shorter events, 0.1 us)
Async XLA Ops:
  7.2 1.5 copy-start
  7.2 23.0 %copy-start.1 = (f32[256,1024]{1,0:T(8,128)S(1)}, f32[256,1024]{1,0:T(8,128)}, u32[]{:S(2)}) copy-start(f32[256,1024]{1,0:T(8,128)} %param.8) | copy-start | bytes 3145732
  7.2 60.3 %reduce-scatter.2.cloned.1.call-start = ((), (), s32[]{:S(2)}) async-start(), calls=%async_computation.1 | async-start | bytes 1310720 | tf_op jit(solution)/shard_map/reduce_scatter | solution.py:34
  9.5 11.4 %collective-permute-start = (f32[64,1024]{1,0:T(8,128)S(1)}, f32[64,1024]{1,0:T(8,128)S(1)}, u32[]{:S(2)}, u32[]{:S(2)}) collective-permute-start(f32[64,1024]{1,0:T(8,128)S(1)} %broadcast_select_fusion), channel_id=1, source_target_pairs={{0,1},{1,2},{2,3},{3,0},{4,5},{5,6},{6,7},{7,4},{8,9},{9,10},{10,1... | collective-permute-start | bytes 786440 | tf_op jit(solution)/shard_map/ppermute | solution.py:19
  20.9 9.3 %collective-permute-start.1 = (f32[64,1024]{1,0:T(8,128)S(1)}, f32[64,1024]{1,0:T(8,128)S(1)}, u32[]{:S(2)}, u32[]{:S(2)}) collective-permute-start(f32[64,1024]{1,0:T(8,128)S(1)} %collective-permute-done), channel_id=1, source_target_pairs={{0,1},{1,2},{2,3},{3,0},{4,5},{5,6},{6,7},{7,4},{8,9},{9,10},{10,1... | collective-permute-start | bytes 786440 | tf_op jit(solution)/shard_map/ppermute | solution.py:19
  30.2 8.4 %collective-permute-start.2 = (f32[64,1024]{1,0:T(8,128)S(1)}, f32[64,1024]{1,0:T(8,128)S(1)}, u32[]{:S(2)}, u32[]{:S(2)}) collective-permute-start(f32[64,1024]{1,0:T(8,128)S(1)} %collective-permute-done.1), channel_id=1, source_target_pairs={{0,1},{1,2},{2,3},{3,0},{4,5},{5,6},{6,7},{7,4},{8,9},{9,10},{10,1... | collective-permute-start | bytes 786440 | tf_op jit(solution)/shard_map/ppermute | solution.py:19
  38.9 1.3 copy-start.2
  40.2 27.3 %copy-start.3 = (f32[256,256]{1,0:T(8,128)}, f32[256,256]{1,0:T(8,128)S(1)}, u32[]{:S(2)}) copy-start(f32[256,256]{1,0:T(8,128)S(1)} %fusion.3) | copy-start | bytes 786436
  42.3 80.7 %all-reduce.2.cloned.1.call-start = ((), (), s32[]{:S(2)}) async-start(), calls=%async_computation.2 | async-start | bytes 524288 | tf_op jit(solution)/shard_map/psum | solution.py:42
  69.0 77.5 %copy-start.4 = (f32[256,256]{1,0:T(8,128)S(1)}, f32[256,256]{1,0:T(8,128)}, u32[]{:S(2)}) copy-start(f32[256,256]{1,0:T(8,128)} %copy-done.3) | copy-start | bytes 786436
  124.1 25.2 %copy-start.5 = (f32[64,1000]{1,0:T(8,128)}, f32[64,1000]{1,0:T(8,128)S(1)}, u32[]{:S(2)}) copy-start(f32[64,1000]{1,0:T(8,128)S(1)} %select_subtract_fusion) | copy-start | bytes 768004
Sparse Core Ops, SparseCore 0:
  42.4 25.0 reduce-scatter.1
  70.5 52.3 all-reduce.1
